TPU v7x, 32 devices: a whole 2x2x4 slice. The times are simulated.
32 devices in a mesh: wide: 4 (over z), narrow: 8 (over y, x, core).
Axes of the slice: x: 2, y: 2, z: 4, core: 2. Of those that a mesh axis runs over, the one named last changes fastest.
Arguments:
- saved_inputs: bfloat16 [1024, 5120], P('wide', 'narrow'), may hold values from -6 to 6
- out_grads: bfloat16 [1024, 5120], P('wide', 'narrow'), may hold values from -48 to 48
- seq_ids: int32 [1024], P('wide'), may hold values from 0 to 7, as said below
- seq_counts: int32 [8], P('wide'), may hold values from 64 to 192, as said below
- basis_in: bfloat16 [5120, 5120], P('narrow'), may hold values from -0.078125 to 0.078125
- basis_out: bfloat16 [5120, 5120], P('narrow'), may hold values from -0.078125 to 0.078125
- query_rotated: bfloat16 [5120, 5120], P('narrow', 'wide'), may hold values from -6 to 6
- damping: float32 [], replicated, may hold values from 0.05 to 0.5
Outputs:
- eigenvalues: float32 [5120, 5120], P('narrow', 'wide')
- preconditioned: float32 [5120, 5120], P('narrow', 'wide')
Inputs may be any that keep to these rules, and one draw needn't show every extreme that they name: seq_ids names for each token its sequence; the 256 tokens of block w of the token axis belong to the sequences 2 * w to 2 * w + 1, each having at least one token. seq_counts[s] is the number of tokens whose seq_ids equal s.
All inputs are finite; a program needn't handle non-finite values.
Results may differ from a plain program's by a relative error of at most 0.01.
Values may be sent and summed in bfloat16 or wider, within the bound.
No kernel may reach another device: no remote copies, remote signals or barrier semaphores. Data moves between devices by JAX's collectives and lax.ppermute only.
A program may use at most 128 MiB of HBM per device.

v0:
```python
import jax
import jax.numpy as jnp
from jax import lax
from jax.sharding import PartitionSpec as P


def shards(
    saved_inputs, out_grads, seq_ids, seq_counts, basis_in, basis_out, query_rotated, damping
):
    part_in = jnp.dot(saved_inputs, basis_in, preferred_element_type=jnp.float32)
    part_grad = jnp.dot(out_grads, basis_out, preferred_element_type=jnp.float32)
    rot_in = lax.psum(part_in, "narrow").astype(jnp.bfloat16)
    rot_grad = lax.psum_scatter(part_grad, "narrow", scatter_dimension=1, tiled=True).astype(
        jnp.bfloat16
    )
    seq_local = seq_counts.shape[0]
    tok_local = seq_ids.shape[0]
    offset = lax.axis_index("wide") * seq_local
    member = seq_ids[None, :] - offset == jnp.arange(seq_local, dtype=jnp.int32)[:, None]
    weight = (
        jnp.where(member, 1.0, 0.0).astype(jnp.float32) / seq_counts.astype(jnp.float32)[:, None]
    )
    weighted = (rot_grad.astype(jnp.float32)[None, :, :] * weight[:, :, None]).astype(jnp.bfloat16)
    total_seqs = seq_local * lax.axis_size("wide")
    groups = lax.axis_size("wide")
    all_weighted = lax.all_gather(weighted, "wide", axis=0, tiled=True)
    all_weighted = all_weighted.reshape(groups, seq_local, tok_local, all_weighted.shape[2])
    column_rows = lax.all_to_all(rot_in, "wide", split_axis=1, concat_axis=0, tiled=True)
    column_rows = column_rows.reshape(groups, tok_local, column_rows.shape[1])
    per_seq = jnp.einsum(
        "gsti,gtj->gsij", all_weighted, column_rows, preferred_element_type=jnp.float32
    )
    eigenvalues = jnp.sum(per_seq * per_seq, axis=(0, 1)) / total_seqs
    scaled = (query_rotated.astype(jnp.float32) / (eigenvalues + damping)).astype(jnp.bfloat16)
    width = query_rotated.shape[1]
    in_columns = lax.dynamic_slice_in_dim(basis_in, lax.axis_index("wide") * width, width, 1)
    all_scaled, all_columns = (
        lax.all_gather(scaled, "narrow", axis=0, tiled=True),
        lax.all_gather(in_columns, "narrow", axis=0, tiled=True),
    )
    middle = jnp.dot(basis_out, all_scaled, preferred_element_type=jnp.float32).astype(jnp.bfloat16)
    partial_back = lax.dot_general(
        middle, all_columns, (((1,), (1,)), ((), ())), preferred_element_type=jnp.float32
    )
    preconditioned = lax.psum_scatter(partial_back, "wide", scatter_dimension=1, tiled=True)
    return (eigenvalues, preconditioned)


def solution(mesh):
    return jax.shard_map(
        shards,
        mesh=mesh,
        in_specs=(
            P("wide", "narrow"),
            P("wide", "narrow"),
            P("wide"),
            P("wide"),
            P("narrow", None),
            P("narrow", None),
            P("narrow", "wide"),
            P(),
        ),
        out_specs=(P("narrow", "wide"), P("narrow", "wide")),
        check_vma=False,
    )
```

profile of v0, /device:TPU:0, one launch (start us, length us, event | category | flops | bytes accessed | tf_op | source)
XLA Modules:
  0.0 662.8 jit_solution(4311589889708317204)
XLA Ops:
  7.2 0.0 copy-start
  7.2 0.0 reduce-scatter.3.cloned.1.call-start
  7.2 0.9 copy-done
  8.1 7.4 %fusion.3 = f32[256,5120]{1,0:T(8,128)} fusion(bf16[256,640]{1,0:T(8,128)(2,1)S(1)} %copy-done, bf16[640,5120]{1,0:T(8,128)(2,1)} %param.13), kind=kOutput, calls=%fused_computation.13 | convolution fusion | flops 1677721600 | bytes 12124160 | tf_op jit(solution)/shard_map/dot_general | solution.py:11
  15.5 0.0 copy-start.3
  15.5 0.0 reduce-scatter.3.cloned.1.call-update
  15.5 0.9 copy-done.3
  16.5 7.4 %fusion.4 = f32[256,5120]{1,0:T(8,128)} fusion(bf16[256,640]{1,0:T(8,128)(2,1)S(1)} %copy-done.3, bf16[640,5120]{1,0:T(8,128)(2,1)} %param.12), kind=kOutput, calls=%fused_computation.14 | convolution fusion | flops 1677721600 | bytes 12124160 | tf_op jit(solution)/shard_map/dot_general | solution.py:10
  23.9 130.5 %all-reduce.1 = bf16[256,5120]{1,0:T(8,128)(2,1)S(1)} all-reduce(f32[256,5120]{1,0:T(8,128)} %fusion.4), channel_id=1, replica_groups=mesh['wide'=4,'narrow'=8] {'narrow'}, use_global_device_ids=true, to_apply=%region_1.0 | all-reduce | flops 1310720 | bytes 7864320 | tf_op jit(solution)/shard_map/psum | solution.py:12
  154.3 1.7 copy.17
  156.0 0.0 copy-start.5
  156.0 0.0 copy-start.4
  156.0 5.1 all-to-all-start
  161.1 0.0 all-gather.4.cloned.1.call-start
  161.1 0.0 copy-done.5
  161.1 0.0 copy-done.4
  161.1 0.1 fusion.2
  161.2 0.0 reduce-scatter.3.cloned.1.call-done
  161.2 1.1 convert_convert_fusion
  162.3 1.0 multiply_convert_fusion
  163.3 0.0 all-gather.4.cloned.1.call-update
  163.3 0.0 all-gather.6.cloned.1.call-start
  164.0 97.9 %all-to-all-done = bf16[256,4,1280]{2,0,1:T(8,128)(2,1)S(1)} async-done(((bf16[256,4,1280]{2,0,1:T(8,128)(2,1)}), bf16[256,4,1280]{2,0,1:T(8,128)(2,1)S(1)}, u32[]{:S(2)}, u32[]{:S(2)}) %all-to-all-start) | async-done | bytes 2621472 | tf_op jit(solution)/shard_map/all_to_all | solution.py:28
  261.9 0.0 all-gather.4.cloned.1.call-done
  261.9 0.0 copy-start.2
  261.9 6.7 %multiply_reduce_fusion = f32[640,1280]{1,0:T(8,128)S(1)} fusion(bf16[4,2,256,640]{3,2,1,0:T(8,128)(2,1)} %bitcast.30, bf16[256,4,1280]{2,0,1:T(8,128)(2,1)S(1)} %all-to-all-done), kind=kOutput, calls=%fused_computation | convolution fusion | flops 3367731200 | bytes 8519680 | tf_op jit(solution)/shard_map/gsti,gtj->gsij/dot_general | solution.py:30
  268.6 0.0 copy-done.2
  268.6 2.9 divide_convert_fusion
  271.5 0.0 all-gather.6.cloned.1.call-update
  271.5 0.0 all-gather.8.cloned.1.call-start
  271.5 2.7 constant_dynamic-slice_fusion
  274.2 0.0 all-gather.8.cloned.1.call-update
  274.3 0.2 reduce-scatter.5.cloned.1.call-start
  274.5 70.8 %all-gather.6.cloned.1.call-done = bf16[5120,1280]{1,0:T(8,128)(2,1)} async-done(((bf16[640,1280]{1,0:T(8,128)(2,1)}), bf16[5120,1280]{1,0:T(8,128)(2,1)}) %all-gather.6.cloned.1.call-update) | async-done | bytes 13107216 | tf_op jit(solution)/shard_map/all_gather | solution.py:38
  345.3 15.3 %convolution_convert_fusion.clone.4 = bf16[1280,640]{1,0:T(8,128)(2,1)S(1)} fusion(bf16[5120,1280]{1,0:T(8,128)(2,1)} %all-gather.6.cloned.1.call-done, bf16[640,5120]{1,0:T(8,128)(2,1)} %param.13), kind=kOutput, calls=%fused_computation.2.clone.clone.clone.1 | convolution fusion | flops 8389427200 | bytes 21299200 | tf_op jit(solution)/shard_map/dot_general | solution.py:41
  360.6 60.7 %all-gather.8.cloned.1.call-done = bf16[5120,1280]{1,0:T(8,128)(2,1)} async-done(((bf16[640,1280]{1,0:T(8,128)(2,1)}), bf16[5120,1280]{1,0:T(8,128)(2,1)}) %all-gather.8.cloned.1.call-update) | async-done | bytes 13107216 | tf_op jit(solution)/shard_map/all_gather | solution.py:39
  421.2 14.5 %fusion.1 = f32[640,5120]{1,0:T(8,128)} fusion(bf16[5120,1280]{1,0:T(8,128)(2,1)} %all-gather.8.cloned.1.call-done, bf16[1280,640]{1,0:T(8,128)(2,1)S(1)} %convolution_convert_fusion.clone.4), kind=kOutput, calls=%fused_computation.5 | convolution fusion | flops 8388608000 | bytes 27852800 | tf_op jit(solution)/shard_map/dot_general | solution.py:42
  435.8 0.0 reduce-scatter.5.cloned.1.call-update
  435.8 0.0 copy-start.1
  435.8 220.5 %reduce-scatter.5.cloned.1.call-done = f32[640,1280]{1,0:T(8,128)} async-done(((f32[640,5120]{1,0:T(8,128)}), f32[640,1280]{1,0:T(8,128)}) %reduce-scatter.5.cloned.1.call-update) | async-done | bytes 3276816 | tf_op jit(solution)/shard_map/reduce_scatter | solution.py:45
  656.3 0.0 copy-done.1
  (2 shorter events, 0.0 us)
Async XLA Ops:
  7.2 1.0 copy-start
  7.2 154.0 %reduce-scatter.3.cloned.1.call-start = ((), (), s32[]{:S(2)}) async-start(), calls=%async_computation.3 | async-start | bytes 5898240 | tf_op jit(solution)/shard_map/reduce_scatter | solution.py:13
  15.5 1.0 copy-start.3
  156.0 5.1 copy-start.5
  156.0 5.1 copy-start.4
  156.0 105.9 %all-to-all-start = ((bf16[256,4,1280]{2,0,1:T(8,128)(2,1)}), bf16[256,4,1280]{2,0,1:T(8,128)(2,1)S(1)}, u32[]{:S(2)}, u32[]{:S(2)}) async-start(bf16[256,4,1280]{2,0,1:T(8,128)(2,1)} %bitcast.28), calls=%async_computation.1 | async-start | bytes 5242880 | tf_op jit(solution)/shard_map/all_to_all | solution.py:28
  161.1 100.8 %all-gather.4.cloned.1.call-start = ((), (), s32[]{:S(2)}) async-start(), calls=%async_computation.4 | async-start | bytes 3276800 | tf_op jit(solution)/shard_map/all_gather | solution.py:26
  163.3 181.9 %all-gather.6.cloned.1.call-start = ((), (), s32[]{:S(2)}) async-start(), calls=%async_computation.5 | async-start | bytes 14745600 | tf_op jit(solution)/shard_map/all_gather | solution.py:38
  261.9 6.7 %copy-start.2 = (bf16[640,1280]{1,0:T(8,128)(2,1)S(1)}, bf16[640,1280]{1,0:T(8,128)(2,1)}, u32[]{:S(2)}) copy-start(bf16[640,1280]{1,0:T(8,128)(2,1)} %param.14) | copy-start | bytes 4915204
  271.5 149.8 %all-gather.8.cloned.1.call-start = ((), (), s32[]{:S(2)}) async-start(), calls=%async_computation.6 | async-start | bytes 14745600 | tf_op jit(solution)/shard_map/all_gather | solution.py:39
  274.3 382.0 %reduce-scatter.5.cloned.1.call-start = ((), (), s32[]{:S(2)}) async-start(), calls=%async_computation.7 | async-start | bytes 16384000 | tf_op jit(solution)/shard_map/reduce_scatter | solution.py:45
  435.8 220.5 %copy-start.1 = (bf16[256,640]{1,0:T(8,128)(2,1)S(1)}, bf16[256,640]{1,0:T(8,128)(2,1)}, u32[]{:S(2)}) copy-start(bf16[256,640]{1,0:T(8,128)(2,1)} %param.9) | copy-start | bytes 983044
Sparse Core Ops, SparseCore 0:
  15.7 80.4 reduce-scatter.2
  164.0 92.1 all-gather.3
  271.6 73.6 all-gather.5
  347.0 74.1 all-gather.7
  435.9 220.3 reduce-scatter.4
where the time goes:
time: 663 us
  waiting for transfers between devices  450 us (68%)
  blocking collectives  130 us (20%)
  matrix products  51.3 us (8%)
  between operations  14.5 us (2%)
    reduce_scatter x1, waiting for transfers between devices, shards(): lax.psum_scatter(partial_back, 'wide', scatter_dimension=1, tiled=True)  220 us
    psum x1, blocking collectives, shards(): rot_in = lax.psum(part_in, 'narrow').astype(jnp.bfloat16)  130 us
    all_to_all x1, waiting for transfers between devices, shards(): lax.all_to_all(rot_in, 'wide', split_axis=1, concat_axis=0, tiled=True)  97.9 us
    all_gather x1, waiting for transfers between devices, shards(): lax.all_gather(scaled, 'narrow', axis=0, tiled=True)  70.8 us
    all_gather x1, waiting for transfers between devices, shards(): lax.all_gather(in_columns, 'narrow', axis=0, tiled=True)  60.7 us
    dot_general x1, matrix products, shards(): jnp.dot(basis_out, all_scaled, preferred_element_type=jnp.float32)  15.3 us
    dot_general x1, matrix products, shards(): lax.dot_general(middle, all_columns, (((1,), (1,)), ((), ())), preferred_...  14.5 us
  transfers between devices with their start and end apart: 6, of which 4 were waited for; matrix products, arithmetic and copies ran while one was open for 4% of the time, Pallas kernels for 0%

commit v1 on v0

--- a/solution.py
+++ b/solution.py
@@ -2,6 +2,10 @@
 import jax.numpy as jnp
 from jax import lax
 from jax.sharding import PartitionSpec as P
+
+
+def step_on_digits(w_in, named_axis):
+    return jax.lax.all_gather(w_in, axis_name=named_axis).sum(axis=0)
 
 
 def shards(
@@ -9,7 +13,7 @@
 ):
     part_in = jnp.dot(saved_inputs, basis_in, preferred_element_type=jnp.float32)
     part_grad = jnp.dot(out_grads, basis_out, preferred_element_type=jnp.float32)
-    rot_in = lax.psum(part_in, "narrow").astype(jnp.bfloat16)
+    rot_in = step_on_digits(part_in, "narrow").astype(jnp.bfloat16)
     rot_grad = lax.psum_scatter(part_grad, "narrow", scatter_dimension=1, tiled=True).astype(
         jnp.bfloat16
     )

time: 663 us -> 787 us (1.19)
  waiting for transfers between devices: 450 us -> 682 us
  blocking collectives: 130 us -> 0 us
  other arithmetic: 5.06 us -> 21.4 us
    all_gather x0 -> x1, waiting for transfers between devices: none -> 197 us  [step_on_digits(): return jax.lax.all_gather(w_in, axis_name=named_axis).sum(axis=0)]
    psum x1 -> x0, blocking collectives: 130 us -> none  [shards(): rot_in = lax.psum(part_in, 'narrow').astype(jnp.bfloat16)]
    all_to_all x1, waiting for transfers between devices: 97.9 us -> 29.6 us  [shards(): lax.all_to_all(rot_in, 'wide', split_axis=1, concat_axis=0, tiled=True)]
    all_gather x1, waiting for transfers between devices: 0.01 us -> 53.8 us  [shards(): all_weighted = lax.all_gather(weighted, 'wide', axis=0, tiled=True)]
    reduce_scatter x1, waiting for transfers between devices: 0.01 us -> 50.2 us  [shards(): lax.psum_scatter(part_grad, 'narrow', scatter_dimension=1, tiled=True)]
    reduce_sum x0 -> x1, other arithmetic: none -> 16.3 us  [step_on_digits(): return jax.lax.all_gather(w_in, axis_name=named_axis).sum(axis=0)]
  transfers between devices with their start and end apart: 6 -> 7, of which waited for: 4 -> 7; matrix products, arithmetic and copies ran while one was open for 4% -> 6% of each run, Pallas kernels for 0% -> 0%
where the time goes in v1:
time: 787 us; the launch traced here: 786 us
  waiting for transfers between devices  682 us (87%)
  matrix products  51.2 us (7%)
  other arithmetic  21.4 us (3%)
  between operations  14.8 us (2%)
  local copies, waits for them, and re-layouts  12.1 us (2%)
    reduce_scatter x1, waiting for transfers between devices, shards(): lax.psum_scatter(partial_back, 'wide', scatter_dimension=1, tiled=True)  220 us
    all_gather x1, waiting for transfers between devices, step_on_digits(): return jax.lax.all_gather(w_in, axis_name=named_axis).sum(axis=0)  197 us
    all_gather x1, waiting for transfers between devices, shards(): lax.all_gather(scaled, 'narrow', axis=0, tiled=True)  70 us
    all_gather x1, waiting for transfers between devices, shards(): lax.all_gather(in_columns, 'narrow', axis=0, tiled=True)  60.7 us
    all_gather x1, waiting for transfers between devices, shards(): all_weighted = lax.all_gather(weighted, 'wide', axis=0, tiled=True)  53.8 us
    reduce_scatter x1, waiting for transfers between devices, shards(): lax.psum_scatter(part_grad, 'narrow', scatter_dimension=1, tiled=True)  50.2 us
    all_to_all x1, waiting for transfers between devices, shards(): lax.all_to_all(rot_in, 'wide', split_axis=1, concat_axis=0, tiled=True)  29.6 us
    reduce_sum x1, other arithmetic, step_on_digits(): return jax.lax.all_gather(w_in, axis_name=named_axis).sum(axis=0)  16.3 us
  transfers between devices with their start and end apart: 7, of which 7 were waited for; matrix products, arithmetic and copies ran while one was open for 6% of the time, Pallas kernels for 0%

profile of v1, /device:TPU:0, one launch (start us, length us, event | category | flops | bytes accessed | tf_op | source)
XLA Modules:
  0.0 786.1 jit_solution(5458452755797926333)
XLA Ops:
  7.2 0.0 copy-start
  7.2 0.0 reduce-scatter.3.cloned.1.call-start
  7.2 0.9 copy-done
  8.1 7.3 fusion.3
  15.5 0.0 copy-start.3
  15.5 0.0 reduce-scatter.3.cloned.1.call-update
  15.5 0.0 all-gather.12.cloned.1.call-start
  15.5 0.9 copy-done.3
  16.4 7.4 fusion.4
  23.9 0.0 copy-start.5
  23.9 0.0 copy-start.4
  23.9 0.0 all-gather.12.cloned.1.call-update
  23.9 0.0 all-gather.6.cloned.1.call-start
  24.0 0.6 copy-done.5
  24.5 0.0 copy-done.4
  24.6 0.1 fusion.2
  24.7 50.2 %reduce-scatter.3.cloned.1.call-done = f32[256,640]{1,0:T(8,128)} async-done(((f32[256,5120]{1,0:T(8,128)}), f32[256,640]{1,0:T(8,128)}) %reduce-scatter.3.cloned.1.call-update) | async-done | bytes 655376 | tf_op jit(solution)/shard_map/reduce_scatter | solution.py:17
  74.8 1.1 convert_convert_fusion
  75.9 1.0 multiply_convert_fusion
  76.9 0.0 all-gather.6.cloned.1.call-update
  77.0 196.8 %all-gather.12.cloned.1.call-done = f32[2048,5120]{1,0:T(8,128)} async-done(((f32[256,5120]{1,0:T(8,128)}), f32[2048,5120]{1,0:T(8,128)}) %all-gather.12.cloned.1.call-update) | async-done | bytes 41943056 | tf_op jit(solution)/shard_map/all_gather | solution.py:8
  273.8 16.3 %reduce_sum.18 = bf16[256,5120]{1,0:T(8,128)(2,1)S(1)} reduce(f32[8,256,5120]{2,1,0:T(8,128)} %bitcast.27, f32[]{:T(128)} %constant.5.clone.1), dimensions={0}, to_apply=%region_1.0 | reduce | flops 9175040 | bytes 44564484 | tf_op jit(solution)/shard_map/reduce_sum | solution.py:8
  290.1 2.6 copy.14
  292.6 4.4 copy.15
  297.0 4.6 all-to-all-start
  301.6 0.0 all-gather.8.cloned.1.call-start
  302.3 53.8 %all-gather.6.cloned.1.call-done = bf16[8,256,640]{2,1,0:T(8,128)(2,1)} async-done(((bf16[2,256,640]{2,1,0:T(8,128)(2,1)}), bf16[8,256,640]{2,1,0:T(8,128)(2,1)}) %all-gather.6.cloned.1.call-update) | async-done | bytes 2621456 | tf_op jit(solution)/shard_map/all_gather | solution.py:30
  356.1 29.6 %all-to-all-done = bf16[256,4,1280]{2,0,1:T(8,128)(2,1)S(1)} async-done(((bf16[256,4,1280]{2,0,1:T(8,128)(2,1)}), bf16[256,4,1280]{2,0,1:T(8,128)(2,1)S(1)}, u32[]{:S(2)}, u32[]{:S(2)}) %all-to-all-start) | async-done | bytes 2621472 | tf_op jit(solution)/shard_map/all_to_all | solution.py:32
  385.7 0.0 copy-start.2
  385.7 6.7 multiply_reduce_fusion
  392.4 0.0 copy-done.2
  392.4 2.9 divide_convert_fusion
  395.3 0.0 all-gather.8.cloned.1.call-update
  395.3 0.0 all-gather.10.cloned.1.call-start
  395.4 2.7 constant_dynamic-slice_fusion
  398.1 0.0 all-gather.10.cloned.1.call-update
  398.1 0.2 reduce-scatter.5.cloned.1.call-start
  398.3 70.0 %all-gather.8.cloned.1.call-done = bf16[5120,1280]{1,0:T(8,128)(2,1)} async-done(((bf16[640,1280]{1,0:T(8,128)(2,1)}), bf16[5120,1280]{1,0:T(8,128)(2,1)}) %all-gather.8.cloned.1.call-update) | async-done | bytes 13107216 | tf_op jit(solution)/shard_map/all_gather | solution.py:42
  468.3 15.3 %convolution_convert_fusion.clone.4 = bf16[1280,640]{1,0:T(8,128)(2,1)S(1)} fusion(bf16[5120,1280]{1,0:T(8,128)(2,1)} %all-gather.8.cloned.1.call-done, bf16[640,5120]{1,0:T(8,128)(2,1)} %param.13), kind=kOutput, calls=%fused_computation.2.clone.clone.clone.1 | convolution fusion | flops 8389427200 | bytes 21299200 | tf_op jit(solution)/shard_map/dot_general | solution.py:45
  483.6 60.7 %all-gather.10.cloned.1.call-done = bf16[5120,1280]{1,0:T(8,128)(2,1)} async-done(((bf16[640,1280]{1,0:T(8,128)(2,1)}), bf16[5120,1280]{1,0:T(8,128)(2,1)}) %all-gather.10.cloned.1.call-update) | async-done | bytes 13107216 | tf_op jit(solution)/shard_map/all_gather | solution.py:43
  544.3 14.5 %fusion.1 = f32[640,5120]{1,0:T(8,128)} fusion(bf16[5120,1280]{1,0:T(8,128)(2,1)} %all-gather.10.cloned.1.call-done, bf16[1280,640]{1,0:T(8,128)(2,1)S(1)} %convolution_convert_fusion.clone.4), kind=kOutput, calls=%fused_computation.4 | convolution fusion | flops 8388608000 | bytes 27852800 | tf_op jit(solution)/shard_map/dot_general | solution.py:46
  558.8 0.0 reduce-scatter.5.cloned.1.call-update
  558.8 0.0 copy-start.1
  558.8 220.5 %reduce-scatter.5.cloned.1.call-done = f32[640,1280]{1,0:T(8,128)} async-done(((f32[640,5120]{1,0:T(8,128)}), f32[640,1280]{1,0:T(8,128)}) %reduce-scatter.5.cloned.1.call-update) | async-done | bytes 3276816 | tf_op jit(solution)/shard_map/reduce_scatter | solution.py:49
  779.3 0.0 copy-done.1
  (2 shorter events, 0.0 us)
Async XLA Ops:
  7.2 1.0 copy-start
  7.2 67.6 %reduce-scatter.3.cloned.1.call-start = ((), (), s32[]{:S(2)}) async-start(), calls=%async_computation.3 | async-start | bytes 5898240 | tf_op jit(solution)/shard_map/reduce_scatter | solution.py:17
  15.5 1.0 copy-start.3
  15.5 258.3 %all-gather.12.cloned.1.call-start = ((), (), s32[]{:S(2)}) async-start(), calls=%async_computation.8 | async-start | bytes 47185920 | tf_op jit(solution)/shard_map/all_gather | solution.py:8
  23.9 0.7 copy-start.5
  23.9 0.7 copy-start.4
  23.9 332.2 %all-gather.6.cloned.1.call-start = ((), (), s32[]{:S(2)}) async-start(), calls=%async_computation.4 | async-start | bytes 3276800 | tf_op jit(solution)/shard_map/all_gather | solution.py:30
  297.0 88.7 %all-to-all-start = ((bf16[256,4,1280]{2,0,1:T(8,128)(2,1)}), bf16[256,4,1280]{2,0,1:T(8,128)(2,1)S(1)}, u32[]{:S(2)}, u32[]{:S(2)}) async-start(bf16[256,4,1280]{2,0,1:T(8,128)(2,1)} %copy.15), calls=%async_computation.1 | async-start | bytes 5242880 | tf_op jit(solution)/shard_map/all_to_all | solution.py:32
  301.6 166.7 %all-gather.8.cloned.1.call-start = ((), (), s32[]{:S(2)}) async-start(), calls=%async_computation.5 | async-start | bytes 14745600 | tf_op jit(solution)/shard_map/all_gather | solution.py:42
  385.7 6.7 copy-start.2
  395.3 149.0 %all-gather.10.cloned.1.call-start = ((), (), s32[]{:S(2)}) async-start(), calls=%async_computation.6 | async-start | bytes 14745600 | tf_op jit(solution)/shard_map/all_gather | solution.py:43
  398.1 381.2 %reduce-scatter.5.cloned.1.call-start = ((), (), s32[]{:S(2)}) async-start(), calls=%async_computation.7 | async-start | bytes 16384000 | tf_op jit(solution)/shard_map/reduce_scatter | solution.py:49
  558.8 220.5 %copy-start.1 = (bf16[256,640]{1,0:T(8,128)(2,1)S(1)}, bf16[256,640]{1,0:T(8,128)(2,1)}, u32[]{:S(2)}) copy-start(bf16[256,640]{1,0:T(8,128)(2,1)} %param.9) | copy-start | bytes 983044
Sparse Core Ops, SparseCore 0:
  15.6 59.1 reduce-scatter.2
  76.7 196.9 all-gather.11
  275.3 80.6 all-gather.5
  395.4 72.8 all-gather.7
  470.0 74.1 all-gather.9
  558.9 220.3 reduce-scatter.4
